TPU v7x, 256 devices: a whole 4x4x8 slice. The times are simulated.
256 devices in a mesh: post: 64 (over x, z, core), rep: 4 (over y).
Axes of the slice: x: 4, y: 4, z: 8, core: 2. Of those that a mesh axis runs over, the one named last changes fastest.
Arguments:
- split_vectors: bfloat16 [2048, 192, 1024], P('post', None, 'rep'), may hold values from -6 to 6
- split_labels: int32 [2048, 192], P('post'), may hold values from 0 to 1, as said below
- split_lengths: int32 [2048], P('post'), may hold values from 144 to 192
- new_owners: int32 [2048, 2], P('post'), may hold values from 0 to 63, all different within a row; in each aligned block of 32 rows (0 to 31, 32 to 63, ...) at most 2 rows name the same one
- neighbour_ids: int32 [2048, 64], replicated, may hold values from 0 to 511, all different within a row
- resident_vectors: bfloat16 [512, 192, 1024], P('post', None, 'rep'), may hold values from -6 to 6
- resident_centroids: bfloat16 [512, 1024], P('post', 'rep'), may hold values from -1 to 1
- resident_lengths: int32 [512], P('post'), may hold values from 1 to 192
Outputs:
- new_postings: bfloat16 [4096, 2, 96, 1024], P('post', None, None, 'rep')
- new_centroids: float32 [2048, 2, 1024], P('post', None, 'rep')
- rescore: float32 [512, 192], P('post')
Inputs may be any that keep to these rules, and one draw needn't show every extreme that they name: `split_labels`: rows at or past a posting's length carry label 1; each half of a split posting holds between 48 and 96 valid rows, and some split has both halves of exactly 96 rows. `new_owners`: the two halves of a split go to different owners; the halves of the splits of one index of post give at most 2 to any one owner. `neighbour_ids`: each split names 64 different postings.
All inputs are finite; a program needn't handle non-finite values.
Results may differ from a plain program's by a relative error of at most 0.0034.
Values may be sent and summed in bfloat16 or wider, within the bound.
No kernel may reach another device: no remote copies, remote signals or barrier semaphores. Data moves between devices by JAX's collectives and lax.ppermute only.
A program may use at most 128 MiB of HBM per device.

v0:
```python
import math
import jax
import jax.numpy as jnp
from jax import lax
from jax.sharding import PartitionSpec as P

D = 1024
far_value = 1e30


def nearest(best_dist, gathered, piece_start, row_data, row_norm, row_onehot, named_table):
    total_cents = gathered.shape[0]
    for block_start in range(0, total_cents, 512):
        block_width = min(512, total_cents - block_start)
        cent_block = gathered[block_start : block_start + block_width]
        cross = lax.dot_general(
            row_data, cent_block, (((1,), (1,)), ((), ())), preferred_element_type=jnp.float32
        )
        block_norm = jnp.einsum(
            "cd,cd->c", cent_block, cent_block, preferred_element_type=jnp.float32
        )
        distance = row_norm[:, None] - 2.0 * cross + block_norm[None, :]
        named_block = lax.dynamic_slice_in_dim(
            named_table, piece_start + block_start, block_width, 1
        )
        row_hits = jnp.dot(row_onehot, named_block, preferred_element_type=jnp.float32)
        distance = jnp.where(row_hits > 0.5, distance, far_value)
        best_dist = jnp.minimum(best_dist, jnp.min(distance, axis=1))
    return best_dist


def body(
    split_vectors,
    split_labels,
    split_lengths,
    new_owners,
    neighbour_ids,
    resident_vectors,
    resident_centroids,
    resident_lengths,
):
    n_post = lax.axis_size("post")
    s_local, length, dim_share = split_vectors.shape
    half_rows = length // 2
    hslot = max(2, 4 * s_local // n_post)
    row_ids = jnp.arange(length)
    is_valid = row_ids[None, :] < split_lengths[:, None]
    in_half = is_valid[:, None, :] & (split_labels[:, None, :] == jnp.arange(2)[None, :, None])
    member_int = in_half.astype(jnp.int32)
    half_rank = jnp.cumsum(member_int, axis=2) - member_int
    placement = in_half[:, :, None, :] & (
        half_rank[:, :, None, :] == jnp.arange(half_rows)[None, None, :, None]
    )
    packed = jnp.einsum(
        "shkr,srd->shkd",
        placement.astype(jnp.bfloat16),
        split_vectors,
        preferred_element_type=jnp.float32,
    ).astype(jnp.bfloat16)
    half_sums = jnp.einsum(
        "shr,srd->shd",
        in_half.astype(jnp.bfloat16),
        split_vectors,
        preferred_element_type=jnp.float32,
    )
    counts = jnp.sum(member_int, axis=2).astype(jnp.float32)
    new_centroids = half_sums / counts[:, :, None]
    owner_flat = new_owners.reshape(-1)
    half_order = jnp.arange(2 * s_local)
    same_owner = (owner_flat[:, None] == owner_flat[None, :]) & (
        half_order[None, :] < half_order[:, None]
    )
    slot_within = jnp.sum(same_owner.astype(jnp.int32), axis=1)
    target_slot = owner_flat * hslot + slot_within
    route_table = (jnp.arange(n_post * hslot)[:, None] == target_slot[None, :]).astype(jnp.bfloat16)
    outgoing = jnp.dot(
        route_table,
        packed.reshape(2 * s_local, half_rows * dim_share),
        preferred_element_type=jnp.float32,
    )
    outgoing = outgoing.astype(jnp.bfloat16).reshape(n_post, hslot, half_rows, dim_share)
    new_postings = lax.all_to_all(outgoing, "post", split_axis=0, concat_axis=0, tiled=True)
    res_local = resident_vectors.shape[0]
    own_diff = (
        resident_vectors.astype(jnp.float32) - resident_centroids.astype(jnp.float32)[:, None, :]
    )
    own_dist = lax.psum(jnp.sum(own_diff * own_diff, axis=2), "rep").reshape(-1)
    post_index = lax.axis_index("post")
    my_postings = post_index * res_local + jnp.arange(res_local)
    hits = jnp.any(neighbour_ids[:, :, None] == my_postings[None, None, :], axis=1)
    named_table = jnp.repeat(hits, 2, axis=0).T.astype(jnp.bfloat16)
    flat_rows = resident_vectors.reshape(res_local * length, dim_share)
    row_data = lax.all_gather(flat_rows, "rep", axis=1, tiled=True)
    row_posting = jnp.arange(res_local * length) // length
    row_norm = jnp.einsum("rd,rd->r", row_data, row_data, preferred_element_type=jnp.float32)
    row_onehot = (row_posting[:, None] == jnp.arange(res_local)[None, :]).astype(jnp.bfloat16)
    centroid_b = new_centroids.astype(jnp.bfloat16).reshape(2 * s_local, dim_share)
    all_shares = lax.all_gather(centroid_b, "post", axis=0, tiled=True)
    all_cents = lax.all_gather(all_shares, "rep", axis=1, tiled=True)
    best_dist = nearest(own_dist, all_cents, 0, row_data, row_norm, row_onehot, named_table)
    scores = (best_dist - row_norm) / math.sqrt(D)
    scores = scores.reshape(res_local, length)
    rescore = jnp.where(row_ids[None, :] < resident_lengths[:, None], scores, 0.0)
    return (new_postings, new_centroids, rescore)


def solution(mesh):
    return jax.shard_map(
        body,
        mesh=mesh,
        in_specs=(
            P("post", None, "rep"),
            P("post", None),
            P("post"),
            P("post", None),
            P(),
            P("post", None, "rep"),
            P("post", "rep"),
            P("post"),
        ),
        out_specs=(P("post", None, None, "rep"), P("post", None, "rep"), P("post", None)),
        check_vma=False,
    )
```

profile of v0, /device:TPU:1, one launch (start us, length us, event | category | flops | bytes accessed | tf_op | source)
XLA Modules:
  0.0 285.8 jit_solution(10616545221353187106)
XLA Ops:
  9.1 1.2 fusion.101
  11.8 1.2 reduce-window.6
  13.4 1.6 fusion.39
  15.0 1.9 copy.83
  17.3 75.5 %all-gather.6.cloned.1.call-done = bf16[4096,256]{1,0:T(8,128)(2,1)} async-done(((bf16[64,256]{1,0:T(8,128)(2,1)}), bf16[4096,256]{1,0:T(8,128)(2,1)}) %all-gather.6.cloned.1.call-update) | async-done | bytes 2097168 | tf_op jit(solution)/shard_map/all_gather | solution.py:98
  92.9 1.8 convolution_convert_fusion
  94.7 4.6 %copy.84 = bf16[16,8,96,256]{3,2,1,0:T(8,128)(2,1)} copy(bf16[16,8,96,256]{3,1,2,0:T(8,128)(2,1)S(1)} %bitcast.85) | data formatting | bytes 12582912
  99.3 7.0 %all-to-all-start = ((bf16[64,2,96,256]{3,2,1,0:T(8,128)(2,1)}), bf16[64,2,96,256]{3,2,1,0:T(8,128)(2,1)}, u32[]{:S(2)}, u32[]{:S(2)}) async-start(bf16[64,2,96,256]{3,2,1,0:T(8,128)(2,1)} %bitcast.84), calls=%async_computation | async-start | bytes 12582912 | tf_op jit(solution)/shard_map/all_to_all | solution.py:82
  107.4 1.0 broadcast_in_dim.15
  108.4 1.3 reshape.111
  110.2 9.5 %psum.7 = f32[1536]{0:T(1024)S(1)} all-reduce(f32[1536]{0:T(1024)S(1)} %reshape.110), channel_id=1, replica_groups=mesh['post'=64,'rep'=4] {'rep'}, use_global_device_ids=true, to_apply=%region_5.6 | all-reduce | flops 1536 | bytes 12288 | tf_op jit(solution)/shard_map/psum | solution.py:87
  119.7 2.4 fusion.75
  122.1 2.3 fusion.74
  124.4 2.3 fusion.73
  126.7 2.3 fusion.72
  129.0 2.4 fusion.71
  131.5 2.4 fusion.70
  133.9 2.4 fusion.69
  136.2 2.3 fusion.68
  138.5 2.7 fusion
  141.3 105.8 %all-to-all-done = bf16[64,2,96,256]{3,2,1,0:T(8,128)(2,1)} async-done(((bf16[64,2,96,256]{3,2,1,0:T(8,128)(2,1)}), bf16[64,2,96,256]{3,2,1,0:T(8,128)(2,1)}, u32[]{:S(2)}, u32[]{:S(2)}) %all-to-all-start) | async-done | bytes 6291488 | tf_op jit(solution)/shard_map/all_to_all | solution.py:82
  247.1 4.4 %fusion.51 = (f32[512]{0:T(512)S(1)}, f32[512]{0:T(512)S(1)}, f32[512]{0:T(512)S(1)}, f32[512]{0:T(512)S(1)}, f32[512]{0:T(512)S(1)}, /*index=5*/f32[512]{0:T(512)S(1)}, f32[512]{0:T(512)S(1)}, f32[512]{0:T(512)S(1)}) fusion(bf16[4096,1024]{1,0:T(8,128)(2,1)} %all-gather.8.cloned.1.call-done), kind=kLoop, calls=%fused_computation.66 | loop fusion | flops 12578816 | bytes 8404992 | tf_op jit(solution)/shard_map/cd,cd->c/dot_general | solution.py:19
  251.5 1.4 copy-done.2
  253.0 4.1 %fusion.52 = f32[1536]{0:T(1024)S(1)} fusion(f32[512]{0:T(512)S(1)} %get-tuple-element.3, bf16[1536,1024]{1,0:T(8,128)(2,1)S(1)} %copy-done.3, f32[1536]{0:T(1024)S(1)} %fusion, f32[1536,512]{0,1:T(8,128)} %fusion.75, bf16[4096,1024]{1,0:T(8,128)(2,1)S(1)} %copy-done.2), kind=kOutput, calls=%fused_computation.68 | convolution fusion | flops 1615329792 | bytes 7356416 | tf_op jit(solution)/shard_map/dot_general | solution.py:16
  257.1 2.1 fusion.53
  259.2 2.1 fusion.54
  261.3 2.1 fusion.55
  263.4 2.1 fusion.56
  265.6 2.1 fusion.57
  267.7 2.3 fusion.58
  270.0 2.1 fusion.59
  272.9 6.5 %copy.93 = bf16[64,2,96,256]{3,2,1,0:T(8,128)(2,1)} copy(bf16[64,2,96,256]{3,2,1,0:T(8,128)(2,1)} %all-to-all-done) | data formatting | bytes 12582912
  (69 shorter events, 6.6 us)
Async XLA Ops:
  7.2 1.9 copy-start
  7.2 85.7 %all-gather.6.cloned.1.call-start = ((), (), s32[]{:S(2)}) async-start(), calls=%async_computation.2 | async-start | bytes 2129920 | tf_op jit(solution)/shard_map/all_gather | solution.py:98
  10.9 127.6 %all-gather.4.cloned.1.call-start = ((), (), s32[]{:S(2)}) async-start(), calls=%async_computation.1 | async-start | bytes 3932160 | tf_op jit(solution)/shard_map/all_gather | solution.py:93
  11.7 235.4 %all-gather.8.cloned.1.call-start = ((), (), s32[]{:S(2)}) async-start(), calls=%async_computation.3 | async-start | bytes 10485760 | tf_op jit(solution)/shard_map/all_gather | solution.py:99
  15.0 2.0 copy-start.14
  99.3 7.0 %copy-start.12 = (s32[2048,64]{0,1:T(8,128)S(1)}, s32[2048,64]{0,1:T(8,128)}, u32[]{:S(2)}) copy-start(s32[2048,64]{0,1:T(8,128)} %param.12) | copy-start | bytes 1572868
  99.3 147.8 %all-to-all-start = ((bf16[64,2,96,256]{3,2,1,0:T(8,128)(2,1)}), bf16[64,2,96,256]{3,2,1,0:T(8,128)(2,1)}, u32[]{:S(2)}, u32[]{:S(2)}) async-start(bf16[64,2,96,256]{3,2,1,0:T(8,128)(2,1)} %bitcast.84), calls=%async_computation | async-start | bytes 12582912 | tf_op jit(solution)/shard_map/all_to_all | solution.py:82
  106.2 3.5 %copy-start.13 = (bf16[8,256]{1,0:T(8,128)(2,1)S(1)}, bf16[8,256]{1,0:T(8,128)(2,1)}, u32[]{:S(2)}) copy-start(bf16[8,256]{1,0:T(8,128)(2,1)} %param.14) | copy-start | bytes 12292
  106.3 3.5 %copy-start.11 = (bf16[8,192,256]{2,1,0:T(8,128)(2,1)S(1)}, bf16[8,192,256]{2,1,0:T(8,128)(2,1)}, u32[]{:S(2)}) copy-start(bf16[8,192,256]{2,1,0:T(8,128)(2,1)} %param.13) | copy-start | bytes 2359300
  138.5 113.0 %copy-start.3 = (bf16[1536,1024]{1,0:T(8,128)(2,1)S(1)}, bf16[1536,1024]{1,0:T(8,128)(2,1)}, u32[]{:S(2)}) copy-start(bf16[1536,1024]{1,0:T(8,128)(2,1)} %all-gather.4.cloned.1.call-done) | copy-start | bytes 9437188
  247.1 5.9 %copy-start.2 = (bf16[4096,1024]{1,0:T(8,128)(2,1)S(1)}, bf16[4096,1024]{1,0:T(8,128)(2,1)}, u32[]{:S(2)}) copy-start(bf16[4096,1024]{1,0:T(8,128)(2,1)} %all-gather.8.cloned.1.call-done) | copy-start | bytes 25165828
  253.0 4.1 %copy-start.10 = (f32[1536,512]{0,1:T(8,128)S(1)}, f32[1536,512]{0,1:T(8,128)}, u32[]{:S(2)}) copy-start(f32[1536,512]{0,1:T(8,128)} %fusion.74) | copy-start | bytes 9437188
  257.1 2.1 copy-start.9
  259.2 2.1 copy-start.8
  261.3 2.1 copy-start.7
  263.4 2.1 copy-start.6
  265.5 2.1 copy-start.5
  267.7 2.3 copy-start.4
  270.0 2.2 copy-start.15
  272.9 6.5 %copy-start.1 = (bf16[32,192,256]{2,1,0:T(8,128)(2,1)S(1)}, bf16[32,192,256]{2,1,0:T(8,128)(2,1)}, u32[]{:S(2)}) copy-start(bf16[32,192,256]{2,1,0:T(8,128)(2,1)} %param.8) | copy-start | bytes 9437188
Sparse Core Ops, SparseCore 0:
  11.4 81.4 all-gather.5
  94.7 42.6 all-gather.3
  139.2 90.3 all-gather.7
where the time goes:
time: 286 us
  waiting for transfers between devices  182 us (64%)
  matrix products  42.2 us (15%)
  local copies, waits for them, and re-layouts  18.6 us (7%)
  between operations  14.2 us (5%)
  other arithmetic  12.2 us (4%)
  blocking collectives  9.52 us (3%)
  starting transfers between devices  7.1 us (2%)
    all_to_all x1, waiting for transfers between devices, body(): lax.all_to_all(outgoing, 'post', split_axis=0, concat_axis=0, tiled=True)  106 us
    all_gather x1, waiting for transfers between devices, body(): all_shares = lax.all_gather(centroid_b, 'post', axis=0, tiled=True)  75.5 us
    dot_general x8, matrix products, nearest(): lax.dot_general(row_data, cent_block, (((1,), (1,)), ((), ())), preferred...  18.9 us
    dot_general x8, matrix products, nearest(): jnp.dot(row_onehot, named_block, preferred_element_type=jnp.float32)  18.8 us
    unnamed x36, local copies, waits for them, and re-layouts  14.6 us
    psum x1, blocking collectives, body(): own_dist = lax.psum(jnp.sum(own_diff * own_diff, axis=2), 'rep').reshape(-1)  9.52 us
    all_to_all x1, starting transfers between devices, body(): lax.all_to_all(outgoing, 'post', split_axis=0, concat_axis=0, tiled=True)  6.98 us
  transfers between devices with their start and end apart: 4, of which 2 were waited for; matrix products, arithmetic and copies ran while one was open for 13% of the time, Pallas kernels for 0%

commit v1 on v0

--- a/solution.py
+++ b/solution.py
@@ -3,6 +3,7 @@
 import jax.numpy as jnp
 from jax import lax
 from jax.sharding import PartitionSpec as P
+from jax.lax import all_to_all, axis_size
 
 D = 1024
 far_value = 1e30
@@ -96,7 +97,11 @@
     row_onehot = (row_posting[:, None] == jnp.arange(res_local)[None, :]).astype(jnp.bfloat16)
     centroid_b = new_centroids.astype(jnp.bfloat16).reshape(2 * s_local, dim_share)
     all_shares = lax.all_gather(centroid_b, "post", axis=0, tiled=True)
-    all_cents = lax.all_gather(all_shares, "rep", axis=1, tiled=True)
+    devs = axis_size("rep")
+    pages = [devs if hop_no == 1 else 1 for hop_no in range(all_shares.ndim)]
+    all_cents = all_to_all(
+        jnp.tile(all_shares, pages), axis_name="rep", split_axis=1, concat_axis=1, tiled=True
+    )
     best_dist = nearest(own_dist, all_cents, 0, row_data, row_norm, row_onehot, named_table)
     scores = (best_dist - row_norm) / math.sqrt(D)
     scores = scores.reshape(res_local, length)

time: 286 us -> 395 us (1.38); the launches traced: 286 us -> 387 us
  waiting for transfers between devices: 182 us -> 249 us
  local copies, waits for them, and re-layouts: 18.6 us -> 42.1 us
  starting transfers between devices: 7.1 us -> 14.2 us
    all_to_all x0 -> x1, waiting for transfers between devices: none -> 106 us  [body(): all_to_all(jnp.tile(all_shares, pages), axis_name='rep', split_axis=1, co...]
    all_to_all x1, waiting for transfers between devices: 106 us -> 60.2 us  [body(): lax.all_to_all(outgoing, 'post', split_axis=0, concat_axis=0, tiled=True)]
    unnamed x36 -> x54, local copies, waits for them, and re-layouts: 14.6 us -> 27.2 us
    all_gather x1, waiting for transfers between devices: 75.5 us -> 82 us  [body(): all_shares = lax.all_gather(centroid_b, 'post', axis=0, tiled=True)]
    all_to_all x0 -> x1, starting transfers between devices: none -> 5.65 us  [body(): all_to_all(jnp.tile(all_shares, pages), axis_name='rep', split_axis=1, co...]
    slice x2 -> x3, local copies, waits for them, and re-layouts: 0.18 us -> 5.8 us  [the longest x1 5.61 us: nearest(): cent_block = gathered[block_start:block_start + block_width]]
    another operation x2 -> x3, local copies, waits for them, and re-layouts: 0.01 us -> 5.35 us  [the longest x1 5.34 us: body(): jnp.tile(all_shares, pages)]
  transfers between devices with their start and end apart: 4 -> 4, of which waited for: 2 -> 3; matrix products, arithmetic and copies ran while one was open for 13% -> 22% of each run, Pallas kernels for 0% -> 0%
where the time goes in v1:
time: 395 us; the launch traced here: 387 us
  waiting for transfers between devices  249 us (63%)
  matrix products  43.4 us (11%)
  local copies, waits for them, and re-layouts  42.1 us (11%)
  between operations  16.2 us (4%)
  starting transfers between devices  14.2 us (4%)
  other arithmetic  14.1 us (4%)
  blocking collectives  7.76 us (2%)
    all_to_all x1, waiting for transfers between devices, body(): all_to_all(jnp.tile(all_shares, pages), axis_name='rep', split_axis=1, co...  106 us
    all_gather x1, waiting for transfers between devices, body(): all_shares = lax.all_gather(centroid_b, 'post', axis=0, tiled=True)  82 us
    all_to_all x1, waiting for transfers between devices, body(): lax.all_to_all(outgoing, 'post', split_axis=0, concat_axis=0, tiled=True)  60.2 us
    unnamed x54, local copies, waits for them, and re-layouts  27.2 us
    dot_general x8, matrix products, nearest(): lax.dot_general(row_data, cent_block, (((1,), (1,)), ((), ())), preferred...  20.1 us
    dot_general x8, matrix products, nearest(): jnp.dot(row_onehot, named_block, preferred_element_type=jnp.float32)  18.8 us
    all_to_all x1, starting transfers between devices, body(): lax.all_to_all(outgoing, 'post', split_axis=0, concat_axis=0, tiled=True)  8.44 us
  transfers between devices with their start and end apart: 4, of which 3 were waited for; matrix products, arithmetic and copies ran while one was open for 22% of the time, Pallas kernels for 0%

profile of v1, /device:TPU:1, one launch (start us, length us, event | category | flops | bytes accessed | tf_op | source)
XLA Modules:
  0.0 386.9 jit_solution(8164489738134917232)
XLA Ops:
  11.8 82.0 %all-gather.5.cloned.1.call-done = bf16[4096,256]{1,0:T(8,128)(2,1)} async-done(((bf16[64,256]{1,0:T(8,128)(2,1)}), bf16[4096,256]{1,0:T(8,128)(2,1)}) %all-gather.5.cloned.1.call-update) | async-done | bytes 2097168 | tf_op jit(solution)/shard_map/all_gather | solution.py:99
  93.7 5.3 %tile.2 = bf16[4096,4,256]{2,0,1:T(8,128)(2,1)} broadcast(bf16[4096,256]{1,0:T(8,128)(2,1)} %all-gather.5.cloned.1.call-done), dimensions={0,2} | broadcast | bytes 10485760 | tf_op jit(solution)/shard_map/tile | solution.py:103
  99.1 5.7 %all-to-all-start.1 = ((bf16[4096,4,256]{2,0,1:T(8,128)(2,1)}), bf16[4096,4,256]{2,0,1:T(8,128)(2,1)}, u32[]{:S(2)}, u32[]{:S(2)}) async-start(bf16[4096,4,256]{2,0,1:T(8,128)(2,1)} %tile.2), calls=%async_computation.1 | async-start | bytes 16777216 | tf_op jit(solution)/shard_map/all_to_all | solution.py:102
  112.7 4.6 %copy.118 = bf16[16,8,96,256]{3,2,1,0:T(8,128)(2,1)} copy(bf16[16,8,96,256]{3,1,2,0:T(8,128)(2,1)S(1)} %bitcast.109) | data formatting | bytes 12582912
  117.3 106.4 %all-to-all-done.1 = bf16[4096,4,256]{2,0,1:T(8,128)(2,1)} async-done(((bf16[4096,4,256]{2,0,1:T(8,128)(2,1)}), bf16[4096,4,256]{2,0,1:T(8,128)(2,1)}, u32[]{:S(2)}, u32[]{:S(2)}) %all-to-all-start.1) | async-done | bytes 8388640 | tf_op jit(solution)/shard_map/all_to_all | solution.py:102
  223.7 8.4 %all-to-all-start = ((bf16[64,2,96,256]{3,2,1,0:T(8,128)(2,1)}), bf16[64,2,96,256]{3,2,1,0:T(8,128)(2,1)}, u32[]{:S(2)}, u32[]{:S(2)}) async-start(bf16[64,2,96,256]{3,2,1,0:T(8,128)(2,1)} %bitcast.108), calls=%async_computation | async-start | bytes 12582912 | tf_op jit(solution)/shard_map/all_to_all | solution.py:83
  236.1 7.8 %psum.7 = f32[1536]{0:T(1024)S(1)} all-reduce(f32[1536]{0:T(1024)S(1)} %reshape.125), channel_id=1, replica_groups=mesh['post'=64,'rep'=4] {'rep'}, use_global_device_ids=true, to_apply=%region_5.6 | all-reduce | flops 1536 | bytes 12288 | tf_op jit(solution)/shard_map/psum | solution.py:88
  243.9 2.3 fusion.67
  246.2 2.3 fusion.66
  248.5 2.4 fusion.65
  250.9 2.3 fusion.64
  253.3 2.4 fusion.63
  255.6 2.3 fusion.62
  257.9 2.4 fusion.61
  260.3 2.4 fusion.60
  262.7 2.6 fusion
  265.3 5.6 %fusion.93 = (bf16[512,4,256]{2,0,1:T(8,128)(2,1)}, bf16[512,4,256]{2,0,1:T(8,128)(2,1)S(1)}, bf16[512,4,256]{2,0,1:T(8,128)(2,1)S(1)}, bf16[512,4,256]{2,0,1:T(...) fusion(bf16[4096,4,256]{2,0,1:T(8,128)(2,1)} %all-to-all-done.1), kind=kLoop, calls=%fused_computation.129 | loop fusion | bytes 16777216 | tf_op jit(solution)/shard_map/slice | solution.py:16
  270.9 2.3 copy.107
  273.2 2.3 copy.108
  275.5 2.3 copy.109
  277.7 2.3 copy.110
  280.0 2.3 copy.111
  291.5 4.3 %fusion.52 = f32[1536]{0:T(1024)S(1)} fusion(f32[512]{0:T(512)S(1)} %fusion.51, bf16[512,1024]{0,1:T(8,128)(2,1)S(1)} %bitcast.118, bf16[1536,1024]{1,0:T(8,128)(2,1)S(1)} %copy-done.8, f32[1536]{0:T(1024)S(1)} %fusion, f32[1536,512]{0,1:T(8,128)} %fusion.67), kind=kOutput, calls=%fused_computation.68 | convolution fusion | flops 1615329792 | bytes 7354368 | tf_op jit(solution)/shard_map/dot_general | solution.py:17
  295.8 2.2 fusion.53
  298.1 2.2 fusion.54
  300.4 2.2 fusion.55
  302.6 2.5 fusion.56
  305.1 2.2 fusion.57
  307.3 2.2 fusion.58
  309.6 2.2 fusion.59
  312.6 60.2 %all-to-all-done = bf16[64,2,96,256]{3,2,1,0:T(8,128)(2,1)} async-done(((bf16[64,2,96,256]{3,2,1,0:T(8,128)(2,1)}), bf16[64,2,96,256]{3,2,1,0:T(8,128)(2,1)}, u32[]{:S(2)}, u32[]{:S(2)}) %all-to-all-start) | async-done | bytes 6291488 | tf_op jit(solution)/shard_map/all_to_all | solution.py:83
  372.8 6.5 %copy.127 = bf16[64,2,96,256]{3,2,1,0:T(8,128)(2,1)} copy(bf16[64,2,96,256]{3,2,1,0:T(8,128)(2,1)} %all-to-all-done) | data formatting | bytes 12582912
  (95 shorter events, 25.4 us)
Async XLA Ops:
  8.0 1.9 copy-start
  8.0 85.7 %all-gather.5.cloned.1.call-start = ((), (), s32[]{:S(2)}) async-start(), calls=%async_computation.3 | async-start | bytes 2129920 | tf_op jit(solution)/shard_map/all_gather | solution.py:99
  99.1 124.6 %all-to-all-start.1 = ((bf16[4096,4,256]{2,0,1:T(8,128)(2,1)}), bf16[4096,4,256]{2,0,1:T(8,128)(2,1)}, u32[]{:S(2)}, u32[]{:S(2)}) async-start(bf16[4096,4,256]{2,0,1:T(8,128)(2,1)} %tile.2), calls=%async_computation.1 | async-start | bytes 16777216 | tf_op jit(solution)/shard_map/all_to_all | solution.py:102
  104.7 158.0 %all-gather.3.cloned.1.call-start = ((), (), s32[]{:S(2)}) async-start(), calls=%async_computation.2 | async-start | bytes 3932160 | tf_op jit(solution)/shard_map/all_gather | solution.py:94
  108.6 2.0 copy-start.19
  223.7 8.5 %copy-start.17 = (s32[2048,64]{0,1:T(8,128)S(1)}, s32[2048,64]{0,1:T(8,128)}, u32[]{:S(2)}) copy-start(s32[2048,64]{0,1:T(8,128)} %param.12) | copy-start | bytes 1572868
  223.7 149.1 %all-to-all-start = ((bf16[64,2,96,256]{3,2,1,0:T(8,128)(2,1)}), bf16[64,2,96,256]{3,2,1,0:T(8,128)(2,1)}, u32[]{:S(2)}, u32[]{:S(2)}) async-start(bf16[64,2,96,256]{3,2,1,0:T(8,128)(2,1)} %bitcast.108), calls=%async_computation | async-start | bytes 12582912 | tf_op jit(solution)/shard_map/all_to_all | solution.py:83
  232.1 3.5 copy-start.18
  232.2 3.5 copy-start.16
  284.9 4.8 %copy-start.4 = (bf16[512,4,256]{0,2,1:T(8,128)(2,1)S(1)}, bf16[512,4,256]{0,2,1:T(8,128)(2,1)}, u32[]{:S(2)}) copy-start(bf16[512,4,256]{0,2,1:T(8,128)(2,1)} %copy.110) | copy-start | bytes 3145732
  284.9 5.2 %copy-start.3 = (bf16[512,4,256]{0,2,1:T(8,128)(2,1)S(1)}, bf16[512,4,256]{0,2,1:T(8,128)(2,1)}, u32[]{:S(2)}) copy-start(bf16[512,4,256]{0,2,1:T(8,128)(2,1)} %copy.111) | copy-start | bytes 3145732
  284.9 5.5 %copy-start.2 = (bf16[512,4,256]{0,2,1:T(8,128)(2,1)S(1)}, bf16[512,4,256]{0,2,1:T(8,128)(2,1)}, u32[]{:S(2)}) copy-start(bf16[512,4,256]{0,2,1:T(8,128)(2,1)} %copy.112) | copy-start | bytes 3145732
  288.1 3.4 copy-start.7
  288.1 3.4 copy-start.8
  291.5 4.3 %copy-start.6 = (bf16[512,4,256]{0,2,1:T(8,128)(2,1)S(1)}, bf16[512,4,256]{0,2,1:T(8,128)(2,1)}, u32[]{:S(2)}) copy-start(bf16[512,4,256]{0,2,1:T(8,128)(2,1)} %copy.108) | copy-start | bytes 3145732
  291.5 4.3 %copy-start.15 = (f32[1536,512]{0,1:T(8,128)S(1)}, f32[1536,512]{0,1:T(8,128)}, u32[]{:S(2)}) copy-start(f32[1536,512]{0,1:T(8,128)} %fusion.66) | copy-start | bytes 9437188
  295.8 2.3 copy-start.5
  295.8 2.3 copy-start.14
  298.1 2.2 copy-start.13
  300.3 2.2 copy-start.12
  302.6 2.5 copy-start.11
  305.1 2.2 copy-start.10
  307.3 2.2 copy-start.9
  309.6 2.3 copy-start.20
  372.8 6.5 %copy-start.1 = (bf16[32,192,256]{2,1,0:T(8,128)(2,1)S(1)}, bf16[32,192,256]{2,1,0:T(8,128)(2,1)}, u32[]{:S(2)}) copy-start(bf16[32,192,256]{2,1,0:T(8,128)(2,1)} %param.8) | copy-start | bytes 9437188
Sparse Core Ops, SparseCore 0:
  12.2 81.4 all-gather.4
Sparse Core Ops, SparseCore 1:
  107.0 70.0 all-gather.2
